TPU v7x, 512 devices: a whole 4x8x8 slice. The times are simulated.
512 devices in a mesh: batch: 16 (over y, core), seq: 32 (over x, z).
Axes of the slice: x: 4, y: 8, z: 8, core: 2. Of those that a mesh axis runs over, the one named last changes fastest.
Arguments:
- tokens: bfloat16 [16, 16384, 768], P('batch', 'seq'), may hold values from -6 to 6
- slide_lengths: int32 [16], P('batch'), may hold values from 2048 to 16384, as said below
- conv_weight: float32 [5, 768], replicated, may hold values from -2.5 to 2.5
- norm_gain: float32 [768], replicated, may hold values from 0.1 to 1.9
- w_query: bfloat16 [768, 768], P('batch'), may hold values from -8 to 8
- w_keyvalue: bfloat16 [768, 1536], P('batch'), may hold values from -0.21875 to 0.21875
- w_out: bfloat16 [768, 768], P('batch'), may hold values from -0.625 to 0.625
Outputs:
- result: bfloat16 [16, 16384, 768], P('batch', 'seq')
Inputs may be any that keep to these rules, and one draw needn't show every extreme that they name: `slide_lengths`: some slide uses all 16384 token slots.
All inputs are finite; a program needn't handle non-finite values.
Results may differ from a plain program's by a relative error of at most 0.0055.
The roundings to bfloat16 on the way count: a program that leaves them out, or rounds other values in their place, can miss the bound.
Values may be sent and summed in bfloat16 or wider, within the bound.
A program may use at most 64 MiB of HBM per device.

v0:
```python
import math
import jax
import jax.numpy as jnp
from jax import lax
from jax.sharding import PartitionSpec as P

HEADS = 12
GROUP = 4
CONV_TAP_COUNT = 5
CONV_DILATION = 3


def with_halo(cells, sides, width):
    for axis, dim in sides:
        count = lax.axis_size(axis)
        ends = count - 1
        head = lax.slice_in_dim(cells, 0, width, axis=dim)
        tail = lax.slice_in_dim(cells, cells.shape[dim] - width, cells.shape[dim], axis=dim)
        cells = jnp.concatenate(
            [
                lax.ppermute(tail, axis, [(i, (i + 1) % count) for i in range(ends)]),
                cells,
                lax.ppermute(head, axis, [((i + 1) % count, i) for i in range(ends)]),
            ],
            axis=dim,
        )
    return cells


def partner_2(block, axis, stride):
    count = lax.axis_size(axis)
    route = []
    for low in range(count):
        high = low | 1 << stride
        if high != low and high < count:
            route += [(low, high), (high, low)]
    return lax.ppermute(block, axis, route)


def start_state(batch_count, row_count, head_size):
    return (
        jnp.full((batch_count, row_count), -1e30, jnp.float32),
        jnp.zeros((batch_count, row_count), jnp.float32),
        jnp.zeros((batch_count, row_count, head_size), jnp.float32),
    )


def absorb(carry_state, query_vectors, key_vectors, value_vectors, usable, part_count):

    def split_parts(array):
        return array.reshape((part_count, array.shape[0] // part_count) + array.shape[1:])

    def update(item_tuple):
        (
            running_max,
            running_sum,
            weighted_values,
            query_segment_block,
            key_segment_block,
            value_block,
            usable_block,
        ) = item_tuple
        score_matrix = jnp.einsum(
            "ftl,fhl->fth",
            query_segment_block,
            key_segment_block,
            preferred_element_type=jnp.float32,
        )
        score_matrix = jnp.where(usable_block[:, None, :], score_matrix, -1000000000.0)
        new_max = jnp.maximum(running_max, jnp.max(score_matrix, axis=-1))
        exponent = jnp.exp(score_matrix - new_max[..., None])
        factor = jnp.exp(running_max - new_max)
        new_sum = running_sum * factor + jnp.sum(exponent, axis=-1)
        new_weighted = weighted_values * factor[..., None] + jnp.einsum(
            "hcp,hpu->hcu",
            exponent.astype(jnp.bfloat16),
            value_block,
            preferred_element_type=jnp.float32,
        )
        return (new_max, new_sum, new_weighted)

    pieces = tuple(
        (
            split_parts(array)
            for array in carry_state + (query_vectors, key_vectors, value_vectors, usable)
        )
    )
    updated = lax.map(update, pieces)
    return tuple((array.reshape((-1,) + array.shape[2:]) for array in updated))


def finish(carry_state):
    running_max, running_sum, weighted_values = carry_state
    return (weighted_values / running_sum[..., None], running_max + jnp.log(running_sum))


def pick_rows(array, rate, head_count):
    grouped = array.reshape(head_count, array.shape[1] // rate, rate, array.shape[2])
    return jnp.stack([grouped[head, :, head % rate, :] for head in range(head_count)])


def spread_rows(outputs, log_total, rate, head_count):
    chosen = jnp.arange(rate)[None, :] == (jnp.arange(head_count) % rate)[:, None]
    full_out = jnp.where(chosen[:, None, :, None], outputs[:, :, None, :], 0.0).reshape(
        head_count, -1, outputs.shape[2]
    )
    full_log = jnp.where(chosen[:, None, :], log_total[:, :, None], -jnp.inf).reshape(
        head_count, -1
    )
    return (full_out, full_log)


def on_device(tokens, slide_lengths, conv_weight, norm_gain, w_query, w_keyvalue, w_out):
    tok_rows = tokens.shape[1]
    model_width = tokens.shape[2]
    head_count = HEADS
    head_size = model_width // head_count
    seq_count = lax.axis_size("seq")
    seq_index = lax.axis_index("seq")
    first_row = seq_index * tok_rows
    length = slide_lengths[0]
    position = first_row + jnp.arange(tok_rows, dtype=jnp.int32)
    live_rows = position < length
    masked = jnp.where(live_rows[:, None], tokens[0], jnp.zeros_like(tokens[0]))
    border_padding = CONV_DILATION * (CONV_TAP_COUNT // 2)
    padded = with_halo(masked, (("seq", 0),), border_padding)
    mixed_rows = masked.astype(jnp.float32)
    for filter_tap_index in range(CONV_TAP_COUNT):
        tap_shift_amount = border_padding + (filter_tap_index - CONV_TAP_COUNT // 2) * CONV_DILATION
        mixed_rows = mixed_rows + conv_weight[filter_tap_index] * padded[
            tap_shift_amount : tap_shift_amount + tok_rows
        ].astype(jnp.float32)
    average = jnp.mean(mixed_rows, axis=-1, keepdims=True)
    centered = mixed_rows - average
    variance = jnp.mean(centered * centered, axis=-1, keepdims=True)
    normed = (centered * lax.rsqrt(variance + 1e-05) * norm_gain).astype(jnp.bfloat16)
    piece_rows = (
        lax.all_gather(w_query, "batch", axis=0, tiled=True),
        lax.all_gather(w_keyvalue, "batch", axis=0, tiled=True),
    )
    columns = normed
    query_sum = jnp.dot(columns, piece_rows[0], preferred_element_type=jnp.float32)
    pair_sum = jnp.dot(columns, piece_rows[1], preferred_element_type=jnp.float32)
    query_vectors = (query_sum * (1.0 / math.sqrt(head_size))).astype(jnp.bfloat16)
    key_value = pair_sum.astype(jnp.bfloat16)
    query_heads = query_vectors.reshape(tok_rows, head_count, head_size).transpose(1, 0, 2)
    key_heads = (
        key_value[:, :model_width].reshape(tok_rows, head_count, head_size).transpose(1, 0, 2)
    )
    value_heads = (
        key_value[:, model_width:].reshape(tok_rows, head_count, head_size).transpose(1, 0, 2)
    )
    head_index = jnp.arange(head_count, dtype=jnp.int32)
    dense_usable = jnp.broadcast_to(live_rows[None, :], (head_count, tok_rows))
    dense_state = absorb(
        start_state(head_count, tok_rows, head_size),
        query_heads,
        key_heads,
        value_heads,
        dense_usable,
        3,
    )
    dense_out, dense_log = finish(dense_state)
    group_rows = tok_rows // GROUP
    group_offsets = head_index % GROUP
    group_queries = pick_rows(query_heads, GROUP, head_count)
    group_block = jnp.stack(
        [pick_rows(key_heads, GROUP, head_count), pick_rows(value_heads, GROUP, head_count)]
    )
    for bit_number in range(GROUP.bit_length() - 1):
        partner = partner_2(group_block, "seq", bit_number)
        upper_half = seq_index >> bit_number & 1 == 1
        group_block = jnp.where(
            upper_half,
            jnp.concatenate([partner, group_block], axis=2),
            jnp.concatenate([group_block, partner], axis=2),
        )
    group_first = seq_index // GROUP * GROUP * tok_rows
    block_steps = GROUP * jnp.arange(GROUP * group_rows, dtype=jnp.int32)
    block_usable = group_first + block_steps[None, :] + group_offsets[:, None] < length
    group_state = absorb(
        start_state(head_count, group_rows, head_size),
        group_queries,
        group_block[0],
        group_block[1],
        block_usable,
        3,
    )
    group_out, group_log = finish(group_state)
    group_out, group_log = spread_rows(group_out, group_log, GROUP, head_count)
    slide_rows = tok_rows // seq_count
    slide_offsets = head_index % seq_count
    slide_queries_own = pick_rows(query_heads, seq_count, head_count)
    slide_keys_own = pick_rows(key_heads, seq_count, head_count)
    slide_values_own = pick_rows(value_heads, seq_count, head_count)
    slide_pairs = jnp.stack([slide_keys_own, slide_values_own])
    piece_rows = lax.all_gather(slide_pairs, "seq", axis=2, tiled=True)
    count = piece_rows.shape[2]
    key_positions = seq_count * jnp.arange(count, dtype=jnp.int32)[None, :] + slide_offsets[:, None]
    slide_state = absorb(
        start_state(head_count, slide_rows, head_size),
        slide_queries_own,
        piece_rows[0],
        piece_rows[1],
        key_positions < length,
        1,
    )
    slide_out, slide_log = finish(slide_state)
    slide_out, slide_log = spread_rows(slide_out, slide_log, seq_count, head_count)
    highest = jnp.maximum(jnp.maximum(dense_log, group_log), slide_log)
    dense_factor = jnp.exp(dense_log - highest)
    group_factor = jnp.exp(group_log - highest)
    slide_factor = jnp.exp(slide_log - highest)
    numer = (
        dense_factor[..., None] * dense_out
        + group_factor[..., None] * group_out
        + slide_factor[..., None] * slide_out
    )
    denom = dense_factor + group_factor + slide_factor
    combined = jnp.where(live_rows[None, :, None], numer / denom[..., None], 0.0)
    attention = combined.transpose(1, 0, 2).reshape(tok_rows, model_width).astype(jnp.bfloat16)
    columns = attention
    projected = jnp.dot(
        columns,
        lax.all_gather(w_out, "batch", axis=0, tiled=True),
        preferred_element_type=jnp.float32,
    )
    return projected.astype(jnp.bfloat16).reshape(1, tok_rows, model_width)


def solution(mesh):
    return jax.shard_map(
        on_device,
        mesh=mesh,
        in_specs=(
            P("batch", "seq", None),
            P("batch"),
            P(),
            P(),
            P("batch", None),
            P("batch", None),
            P("batch", None),
        ),
        out_specs=P("batch", "seq", None),
        check_vma=False,
    )
```

profile of v0, /device:TPU:1, one launch (start us, length us, event | category | flops | bytes accessed | tf_op | source)
XLA Modules:
  0.0 283.2 jit_solution(16786506327512890809)
XLA Ops:
  9.3 4.8 %collective-permute-start = (bf16[6,768]{1,0:T(8,128)(2,1)S(1)}, bf16[6,768]{1,0:T(8,128)(2,1)S(1)}, u32[]{:S(2)}, u32[]{:S(2)}) collective-permute-start(bf16[6,768]{1,0:T(8,128)(2,1)S(1)} %get-tuple-element.344), channel_id=1, source_target_pairs={{0,1},{1,2},{2,3},{3,4},{4,5},{5,6},{6,7},{7,8},{8,9},{9,10},{10,1... | collective-permute-start | bytes 27656 | tf_op jit(solution)/shard_map/ppermute | solution.py:21
  15.6 3.6 %collective-permute-done.1 = bf16[6,768]{1,0:T(8,128)(2,1)S(1)} collective-permute-done((bf16[6,768]{1,0:T(8,128)(2,1)S(1)}, bf16[6,768]{1,0:T(8,128)(2,1)S(1)}, u32[]{:S(2)}, u32[]{:S(2)}) %collective-permute-start.1) | collective-permute-done | bytes 9248 | tf_op jit(solution)/shard_map/ppermute | solution.py:23
  20.7 37.1 %all-gather.7.cloned.1.call-done = bf16[768,1536]{1,0:T(8,128)(2,1)} async-done(((bf16[48,1536]{1,0:T(8,128)(2,1)}), bf16[768,1536]{1,0:T(8,128)(2,1)}) %all-gather.7.cloned.1.call-update) | async-done | bytes 2359312 | tf_op jit(solution)/shard_map/all_gather | solution.py:139
  57.8 3.1 %convolution_convert_fusion = bf16[512,1536]{1,0:T(8,128)(2,1)S(1)} fusion(bf16[768,1536]{1,0:T(8,128)(2,1)} %all-gather.7.cloned.1.call-done, f32[512,768]{1,0:T(8,128)S(1)} %get-tuple-element.253, f32[768]{0:T(1024)S(1)} %copy-done.15, f32[512]{0:T(512)S(1)} %add_rsqrt_fusion, f32[512]{0:T(512)S(1)} %broadcast_multiply_fusion), kind=kOutput, calls=%fused_computation.64 | convolution fusion | flops 1210318848 | bytes 5512192 | tf_op jit(solution)/shard_map/dot_general | solution.py:143
  72.3 27.5 %all-gather.5.cloned.1.call-done = bf16[768,768]{1,0:T(8,128)(2,1)} async-done(((bf16[48,768]{1,0:T(8,128)(2,1)}), bf16[768,768]{1,0:T(8,128)(2,1)}) %all-gather.5.cloned.1.call-update) | async-done | bytes 1179664 | tf_op jit(solution)/shard_map/all_gather | solution.py:138
  99.9 3.0 %multiply_convert_fusion = bf16[512,768]{1,0:T(8,128)(2,1)} fusion(bf16[768,768]{1,0:T(8,128)(2,1)} %all-gather.5.cloned.1.call-done, f32[512,768]{1,0:T(8,128)S(1)} %get-tuple-element.253, f32[768]{0:T(1024)S(1)} %copy-done.15, f32[512]{0:T(512)S(1)} %add_rsqrt_fusion, f32[512]{0:T(512)S(1)} %broadcast_multiply_fusion), kind=kOutput, calls=%fused_computation.72 | convolution fusion | flops 606339072 | bytes 3546112 | tf_op jit(solution)/shard_map/dot_general | solution.py:142
  107.5 2.4 fusion.82
  117.5 2.4 fusion.79
  127.7 3.0 %fusion.81 = (bf16[1,128,1,64]{3,2,1,0:T(2,128)(2,1)S(1)}, bf16[1,128,1,64]{3,2,1,0:T(2,128)(2,1)S(1)}, bf16[1,128,1,64]{3,2,1,0:T(2,128)(2,1)S(1)}, bf16[1,128,...) fusion(bf16[12,128,4,64]{3,2,1,0:T(4,128)(2,1)} %bitcast.349), kind=kLoop, calls=%fused_computation.224 | loop fusion | bytes 393216 | tf_op jit(solution)/shard_map/slice | solution.py:99
  148.3 3.4 %collective-permute-start.2 = (bf16[2,12,128,64]{2,3,1,0:T(8,128)(2,1)S(1)}, bf16[2,12,128,64]{2,3,1,0:T(8,128)(2,1)S(1)}, u32[]{:S(2)}, u32[]{:S(2)}) collective-permute-start(bf16[2,12,128,64]{2,3,1,0:T(8,128)(2,1)S(1)} %pad_maximum_fusion.2), channel_id=1, source_target_pairs={{0,1},{1,0},{2,3},{3,2},{4,5},{5,4},{6,7},{7,6},{8,9},{9,8},{10,11... | collective-permute-start | bytes 1179656 | tf_op jit(solution)/shard_map/ppermute | solution.py:37
  152.3 9.9 %collective-permute-done.2 = bf16[2,12,128,64]{2,3,1,0:T(8,128)(2,1)S(1)} collective-permute-done((bf16[2,12,128,64]{2,3,1,0:T(8,128)(2,1)S(1)}, bf16[2,12,128,64]{2,3,1,0:T(8,128)(2,1)S(1)}, u32[]{:S(2)}, u32[]{:S(2)}) %collective-permute-start.2) | collective-permute-done | bytes 393248 | tf_op jit(solution)/shard_map/ppermute | solution.py:37
  163.4 4.9 %collective-permute-start.3 = (bf16[2,12,256,64]{2,3,1,0:T(8,128)(2,1)}, bf16[2,12,256,64]{2,3,1,0:T(8,128)(2,1)}, u32[]{:S(2)}, u32[]{:S(2)}) collective-permute-start(bf16[2,12,256,64]{2,3,1,0:T(8,128)(2,1)} %maximum_select_fusion.1), channel_id=1, source_target_pairs={{0,2},{2,0},{1,3},{3,1},{4,6},{6,4},{5,7},{7,5},{8,10},{10,8},{9,1... | collective-permute-start | bytes 2359304 | tf_op jit(solution)/shard_map/ppermute | solution.py:37
  168.4 13.2 %while.10 = (s32[]{:T(128)}, f32[3,4,512]{2,1,0:T(4,128)S(1)}, f32[3,4,512]{2,1,0:T(4,128)S(1)}, f32[3,4,512,64]{2,3,1,0:T(8,128)}, pred[3,4,512]{2,1,0:T(4,128)...) while((s32[]{:T(128)}, f32[3,4,512]{2,1,0:T(4,128)S(1)}, ...), condition=%wide.region_5.6_spmd, body=%wide.region_2.5_spmd.sunk | while | flops 276965376 | bytes 14004325 | solution.py:88
  182.9 2.1 copy.1481
  185.0 27.4 %collective-permute-done.3 = bf16[2,12,256,64]{2,3,1,0:T(8,128)(2,1)} collective-permute-done((bf16[2,12,256,64]{2,3,1,0:T(8,128)(2,1)}, bf16[2,12,256,64]{2,3,1,0:T(8,128)(2,1)}, u32[]{:S(2)}, u32[]{:S(2)}) %collective-permute-start.3) | collective-permute-done | bytes 786464 | tf_op jit(solution)/shard_map/ppermute | solution.py:37
  212.3 2.6 maximum_select_fusion
  216.2 11.3 %while.11 = (s32[]{:T(128)}, f32[3,4,128]{2,1,0:T(4,128)S(1)}, f32[3,4,128]{2,1,0:T(4,128)S(1)}, f32[3,4,128,64]{2,3,1,0:T(8,128)}, pred[3,4,512]{2,1,0:T(4,128)...) while((s32[]{:T(128)}, f32[3,4,128]{2,1,0:T(4,128)S(1)}, ...), condition=%wide.region_9.10_spmd, body=%wide.region_6.9_spmd.sunk | while | flops 68717056 | bytes 3899493 | solution.py:88
  217.6 2.0 fusion.111
  225.1 2.0 fusion.111
  230.6 9.3 %fusion.74 = (bf16[1,12,512,64]{3,0,1,2:T(2,128)(2,1)}, bf16[1,12,512,64]{3,0,1,2:T(2,128)(2,1)}) fusion(bf16[2,12,512,64]{3,0,1,2:T(2,128)(2,1)} %all-gather.9.cloned.1.call-done), kind=kLoop, calls=%fused_computation.217 | loop fusion | bytes 3145728 | tf_op jit(solution)/shard_map/slice | solution.py:204
  239.9 7.9 %copy.1535 = bf16[1,12,512,64]{2,3,1,0:T(8,128)(2,1)} copy(bf16[1,12,512,64]{3,0,1,2:T(2,128)(2,1)} %get-tuple-element.267) | data formatting | bytes 1572864
  247.8 7.9 %copy.1536 = bf16[1,12,512,64]{2,3,1,0:T(8,128)(2,1)} copy(bf16[1,12,512,64]{3,0,1,2:T(2,128)(2,1)} %get-tuple-element.266) | data formatting | bytes 1572864
  263.6 8.3 %fusion.52 = bf16[12,512,64]{2,1,0:T(8,128)(2,1)} fusion(f32[12,512,64]{2,1,0:T(8,128)S(1)} %bitcast.338, f32[3,4,512,64]{3,2,1,0:T(8,128)S(1)} %copy.1481, f32[12,512]{1,0:T(8,128)S(1)} %get-tuple-element.248, f32[12,16,64]{2,1,0:T(8,128)S(1)} %fusion.58, f32[12,512]{1,0:T(8,128)S(1)} %get-tuple-element.251, f32[12,512]{1,0:T(8,128)S(1)} %get-tuple-element.249, ...), kind=kLoop, calls=%fused_computation.63 | loop fusion | flops 4325376 | bytes 4116992 | tf_op jit(solution)/shard_map/convert_element_type | solution.py:221
  273.7 3.0 %fusion.57 = bf16[1,512,768]{2,1,0:T(8,128)(2,1)} fusion(bf16[512,768]{0,1:T(8,128)(2,1)S(1)} %bitcast.359, bf16[768,768]{1,0:T(8,128)(2,1)} %all-gather.11.cloned.1.call-done), kind=kOutput, calls=%fused_computation.76 | convolution fusion | flops 604372992 | bytes 2752512 | tf_op jit(solution)/shard_map/dot_general | solution.py:223
  (249 shorter events, 90.8 us)
Async XLA Ops:
  6.5 9.0 %copy-start.9 = (f32[5,768]{1,0:T(8,128)S(1)}, f32[5,768]{1,0:T(8,128)}, u32[]{:S(2)}) copy-start(f32[5,768]{1,0:T(8,128)} %param.13) | copy-start | bytes 46084
  6.5 51.2 %all-gather.7.cloned.1.call-start = ((), (), s32[]{:S(2)}) async-start(), calls=%async_computation.1 | async-start | bytes 2506752 | tf_op jit(solution)/shard_map/all_gather | solution.py:139
  7.3 92.6 %all-gather.5.cloned.1.call-start = ((), (), s32[]{:S(2)}) async-start(), calls=%async_computation | async-start | bytes 1253376 | tf_op jit(solution)/shard_map/all_gather | solution.py:138
  8.0 7.5 %copy-start.12 = (pred[512]{0:T(512)(128)(4,1)}, pred[512]{0:T(512)(128)(4,1)S(1)}, u32[]{:S(2)}) copy-start(pred[512]{0:T(512)(128)(4,1)S(1)} %add_compare_fusion.2) | copy-start | bytes 1540
  9.3 6.3 %collective-permute-start = (bf16[6,768]{1,0:T(8,128)(2,1)S(1)}, bf16[6,768]{1,0:T(8,128)(2,1)S(1)}, u32[]{:S(2)}, u32[]{:S(2)}) collective-permute-start(bf16[6,768]{1,0:T(8,128)(2,1)S(1)} %get-tuple-element.344), channel_id=1, source_target_pairs={{0,1},{1,2},{2,3},{3,4},{4,5},{5,6},{6,7},{7,8},{8,9},{9,10},{10,1... | collective-permute-start | bytes 27656 | tf_op jit(solution)/shard_map/ppermute | solution.py:21
  14.1 5.1 %collective-permute-start.1 = (bf16[6,768]{1,0:T(8,128)(2,1)S(1)}, bf16[6,768]{1,0:T(8,128)(2,1)S(1)}, u32[]{:S(2)}, u32[]{:S(2)}) collective-permute-start(bf16[6,768]{1,0:T(8,128)(2,1)S(1)} %get-tuple-element.345), channel_id=1, source_target_pairs={{1,0},{2,1},{3,2},{4,3},{5,4},{6,5},{7,6},{8,7},{9,8},{10,9},{11,1... | collective-permute-start | bytes 27656 | tf_op jit(solution)/shard_map/ppermute | solution.py:23
  15.4 215.2 %all-gather.9.cloned.1.call-start = ((), (), s32[]{:S(2)}) async-start(), calls=%async_computation.2 | async-start | bytes 3244032 | tf_op jit(solution)/shard_map/all_gather | solution.py:197
  19.2 38.6 %copy-start.15 = (f32[768]{0:T(1024)S(1)}, f32[768]{0:T(1024)}, u32[]{:S(2)}) copy-start(f32[768]{0:T(1024)} %param.14) | copy-start | bytes 9220
  69.9 203.8 %all-gather.11.cloned.1.call-start = ((), (), s32[]{:S(2)}) async-start(), calls=%async_computation.3 | async-start | bytes 1253376 | tf_op jit(solution)/shard_map/all_gather | solution.py:225
  117.4 2.5 copy-start.4
  135.9 16.4 %copy-start.3 = (bf16[1,128,1,64]{1,3,2,0:T(8,128)(2,1)S(1)}, bf16[1,128,1,64]{1,3,2,0:T(8,128)(2,1)}, u32[]{:S(2)}) copy-start(bf16[1,128,1,64]{1,3,2,0:T(8,128)(2,1)} %copy.1434) | copy-start | bytes 49156
  136.6 15.1 %copy-start.6 = (bf16[1,16,1,64]{3,2,1,0:T(2,128)(2,1)S(1)}, bf16[1,16,1,64]{3,2,1,0:T(2,128)(2,1)}, u32[]{:S(2)}) copy-start(bf16[1,16,1,64]{3,2,1,0:T(2,128)(2,1)} %get-tuple-element.292) | copy-start | bytes 6148
  137.3 31.1 %copy-start.13 = (pred[512]{0:T(512)(128)(4,1)S(1)}, pred[512]{0:T(512)(128)(4,1)}, u32[]{:S(2)}) copy-start(pred[512]{0:T(512)(128)(4,1)} %copy-done.12) | copy-start | bytes 1540
  137.3 31.1 %copy-start.7 = (f32[3,4,512]{2,1,0:T(4,128)S(1)}, f32[3,4,512]{2,1,0:T(4,128)}, u32[]{:S(2)}) copy-start(f32[3,4,512]{2,1,0:T(4,128)} %custom-call.6) | copy-start | bytes 73732
  137.3 31.1 %copy-start.8 = (f32[3,4,512]{2,1,0:T(4,128)S(1)}, f32[3,4,512]{2,1,0:T(4,128)}, u32[]{:S(2)}) copy-start(f32[3,4,512]{2,1,0:T(4,128)} %custom-call.7) | copy-start | bytes 73732
  148.3 13.9 %collective-permute-start.2 = (bf16[2,12,128,64]{2,3,1,0:T(8,128)(2,1)S(1)}, bf16[2,12,128,64]{2,3,1,0:T(8,128)(2,1)S(1)}, u32[]{:S(2)}, u32[]{:S(2)}) collective-permute-start(bf16[2,12,128,64]{2,3,1,0:T(8,128)(2,1)S(1)} %pad_maximum_fusion.2), channel_id=1, source_target_pairs={{0,1},{1,0},{2,3},{3,2},{4,5},{5,4},{6,7},{7,6},{8,9},{9,8},{10,11... | collective-permute-start | bytes 1179656 | tf_op jit(solution)/shard_map/ppermute | solution.py:37
  163.4 48.9 %collective-permute-start.3 = (bf16[2,12,256,64]{2,3,1,0:T(8,128)(2,1)}, bf16[2,12,256,64]{2,3,1,0:T(8,128)(2,1)}, u32[]{:S(2)}, u32[]{:S(2)}) collective-permute-start(bf16[2,12,256,64]{2,3,1,0:T(8,128)(2,1)} %maximum_select_fusion.1), channel_id=1, source_target_pairs={{0,2},{2,0},{1,3},{3,1},{4,6},{6,4},{5,7},{7,5},{8,10},{10,8},{9,1... | collective-permute-start | bytes 2359304 | tf_op jit(solution)/shard_map/ppermute | solution.py:37
  214.9 1.3 copy-start.10
  214.9 1.3 copy-start.11
  247.8 7.9 %copy-start.5 = (pred[12,512]{1,0:T(8,128)(4,1)S(1)}, pred[12,512]{1,0:T(8,128)(4,1)}, u32[]{:S(2)}) copy-start(pred[12,512]{1,0:T(8,128)(4,1)} %add_compare_fusion) | copy-start | bytes 18436
  260.4 2.5 copy-start
  262.9 0.8 copy-start.1
  262.9 0.8 copy-start.2
  262.9 0.7 copy-start.14
Sparse Core Ops, SparseCore 0:
  9.5 48.2 all-gather.6
  59.9 39.9 all-gather.4
  103.0 101.3 all-gather.8
  206.4 41.1 all-gather.10
where the time goes:
time: 286 us; the launch traced here: 283 us
  waiting for transfers between devices  107 us (37%)
  local copies, waits for them, and re-layouts  92.1 us (32%)
  matrix products  32.4 us (11%)
  other arithmetic  22.6 us (8%)
  between operations  14.6 us (5%)
  starting transfers between devices  14.5 us (5%)
    unnamed x112, local copies, waits for them, and re-layouts  38.8 us
    ppermute x2, waiting for transfers between devices, partner_2(): return lax.ppermute(block, axis, route)  37.3 us
    all_gather x1, waiting for transfers between devices, on_device(): lax.all_gather(w_keyvalue, 'batch', axis=0, tiled=True)  37.1 us
    all_gather x1, waiting for transfers between devices, on_device(): lax.all_gather(w_query, 'batch', axis=0, tiled=True)  27.5 us
    slice x30, local copies, waits for them, and re-layouts, pick_rows(): grouped[head, :, head % rate, :]  21 us
    dot_general x7, matrix products, update(): jnp.einsum('hcp,hpu->hcu', exponent.astype(jnp.bfloat16), value_block, pr...  13.2 us
    dot_general x7, matrix products, update(): jnp.einsum('ftl,fhl->fth', query_segment_block, key_segment_block, prefer...  10.1 us
    slice x1, local copies, waits for them, and re-layouts, on_device(): piece_rows[1]  9.28 us
  transfers between devices with their start and end apart: 8, of which 5 were waited for; matrix products, arithmetic and copies ran while one was open for 51% of the time, Pallas kernels for 0%

commit v1 on v0

--- a/solution.py
+++ b/solution.py
@@ -8,6 +8,22 @@
 GROUP = 4
 CONV_TAP_COUNT = 5
 CONV_DILATION = 3
+
+
+def ring_gather(x, axis, dim):
+    ways, here, step = (lax.axis_size(axis), lax.axis_index(axis), x.shape[dim])
+    shape = [n * ways if d == dim else n for d, n in enumerate(x.shape)]
+    full = lax.dynamic_update_slice_in_dim(jnp.zeros(shape, x.dtype), x, here * step, axis=dim)
+    going_up = going_down = x
+    for far in range(1, ways // 2 + 1):
+        going_up = lax.ppermute(going_up, axis, [(d, (d + 1) % ways) for d in range(ways)])
+        full = lax.dynamic_update_slice_in_dim(full, going_up, (here - far) % ways * step, axis=dim)
+        if 2 * far < ways:
+            going_down = lax.ppermute(going_down, axis, [(d, (d - 1) % ways) for d in range(ways)])
+            full = lax.dynamic_update_slice_in_dim(
+                full, going_down, (here + far) % ways * step, axis=dim
+            )
+    return full
 
 
 def with_halo(cells, sides, width):
@@ -135,7 +151,7 @@
     variance = jnp.mean(centered * centered, axis=-1, keepdims=True)
     normed = (centered * lax.rsqrt(variance + 1e-05) * norm_gain).astype(jnp.bfloat16)
     piece_rows = (
-        lax.all_gather(w_query, "batch", axis=0, tiled=True),
+        ring_gather(w_query, "batch", 0),
         lax.all_gather(w_keyvalue, "batch", axis=0, tiled=True),
     )
     columns = normed

time: 286 us -> 276 us (0.965)
  waiting for transfers between devices: 107 us -> 73.7 us
  starting transfers between devices: 14.5 us -> 37.5 us
    all_gather x1 -> x0, waiting for transfers between devices: 27.5 us -> none  [on_device(): lax.all_gather(w_query, 'batch', axis=0, tiled=True)]
    ppermute x0 -> x15, starting transfers between devices: none -> 23.8 us  [the longest x7 16.7 us: ring_gather(): lax.ppermute(going_down, axis, [(d, (d - 1) % ways) for d in range(ways)])]
    ppermute x2, waiting for transfers between devices: 37.3 us -> 22.2 us  [partner_2(): return lax.ppermute(block, axis, route)]
    ppermute x0 -> x15, waiting for transfers between devices: none -> 9.92 us  [the longest x8 9.45 us: ring_gather(): lax.ppermute(going_up, axis, [(d, (d + 1) % ways) for d in range(ways)])]
    unnamed x112 -> x114, local copies, waits for them, and re-layouts: 38.8 us -> 38.8 us
  transfers between devices with their start and end apart: 8 -> 22, of which waited for: 5 -> 14; matrix products, arithmetic and copies ran while one was open for 51% -> 48% of each run, Pallas kernels for 0% -> 0%
where the time goes in v1:
time: 276 us; the launch traced here: 273 us
  local copies, waits for them, and re-layouts  92.7 us (34%)
  waiting for transfers between devices  73.7 us (27%)
  starting transfers between devices  37.5 us (14%)
  matrix products  31.1 us (11%)
  other arithmetic  22.4 us (8%)
  between operations  15.1 us (5%)
    unnamed x114, local copies, waits for them, and re-layouts  38.8 us
    all_gather x1, waiting for transfers between devices, on_device(): lax.all_gather(w_keyvalue, 'batch', axis=0, tiled=True)  37.1 us
    ppermute x2, waiting for transfers between devices, partner_2(): return lax.ppermute(block, axis, route)  22.2 us
    slice x30, local copies, waits for them, and re-layouts, pick_rows(): grouped[head, :, head % rate, :]  21.2 us
    ppermute x7, starting transfers between devices, ring_gather(): lax.ppermute(going_down, axis, [(d, (d - 1) % ways) for d in range(ways)])  16.7 us
    dot_general x7, matrix products, update(): jnp.einsum('hcp,hpu->hcu', exponent.astype(jnp.bfloat16), value_block, pr...  13.2 us
    dot_general x7, matrix products, update(): jnp.einsum('ftl,fhl->fth', query_segment_block, key_segment_block, prefer...  10.1 us
    ppermute x8, waiting for transfers between devices, ring_gather(): lax.ppermute(going_up, axis, [(d, (d + 1) % ways) for d in range(ways)])  9.45 us
  transfers between devices with their start and end apart: 22, of which 14 were waited for; matrix products, arithmetic and copies ran while one was open for 48% of the time, Pallas kernels for 0%

profile of v1, /device:TPU:1, one launch (start us, length us, event | category | flops | bytes accessed | tf_op | source)
XLA Modules:
  0.0 272.6 jit_solution(17923962602906898053)
XLA Ops:
  9.3 4.8 %collective-permute-start = (bf16[6,768]{1,0:T(8,128)(2,1)S(1)}, bf16[6,768]{1,0:T(8,128)(2,1)S(1)}, u32[]{:S(2)}, u32[]{:S(2)}) collective-permute-start(bf16[6,768]{1,0:T(8,128)(2,1)S(1)} %get-tuple-element.344), channel_id=1, source_target_pairs={{0,1},{1,2},{2,3},{3,4},{4,5},{5,6},{6,7},{7,8},{8,9},{9,10},{10,1... | collective-permute-start | bytes 27656 | tf_op jit(solution)/shard_map/ppermute | solution.py:37
  15.5 3.7 %collective-permute-done.1 = bf16[6,768]{1,0:T(8,128)(2,1)S(1)} collective-permute-done((bf16[6,768]{1,0:T(8,128)(2,1)S(1)}, bf16[6,768]{1,0:T(8,128)(2,1)S(1)}, u32[]{:S(2)}, u32[]{:S(2)}) %collective-permute-start.1) | collective-permute-done | bytes 9248 | tf_op jit(solution)/shard_map/ppermute | solution.py:39
  20.7 37.1 %all-gather.4.cloned.1.call-done = bf16[768,1536]{1,0:T(8,128)(2,1)} async-done(((bf16[48,1536]{1,0:T(8,128)(2,1)}), bf16[768,1536]{1,0:T(8,128)(2,1)}) %all-gather.4.cloned.1.call-update) | async-done | bytes 2359312 | tf_op jit(solution)/shard_map/all_gather | solution.py:155
  57.8 3.1 %convolution_convert_fusion = bf16[512,1536]{1,0:T(8,128)(2,1)S(1)} fusion(bf16[768,1536]{1,0:T(8,128)(2,1)} %all-gather.4.cloned.1.call-done, f32[512,768]{1,0:T(8,128)S(1)} %get-tuple-element.253, f32[768]{0:T(1024)S(1)} %copy-done.16, f32[512]{0:T(512)S(1)} %add_rsqrt_fusion, f32[512]{0:T(512)S(1)} %broadcast_multiply_fusion), kind=kOutput, calls=%fused_computation.64 | convolution fusion | flops 1210318848 | bytes 5512192 | tf_op jit(solution)/shard_map/dot_general | solution.py:159
  82.8 2.7 %collective-permute-start.9 = (bf16[48,768]{1,0:T(8,128)(2,1)S(1)}, bf16[48,768]{1,0:T(8,128)(2,1)S(1)}, u32[]{:S(2)}, u32[]{:S(2)}) collective-permute-start(bf16[48,768]{1,0:T(8,128)(2,1)S(1)} %collective-permute-done.7), channel_id=1, source_target_pairs={{0,480},{32,0},{64,32},{96,64},{128,96},{160,128},{192,160},{224,1... | collective-permute-start | bytes 221192 | tf_op jit(solution)/shard_map/ppermute | solution.py:22
  86.6 3.9 %collective-permute-start.11 = (bf16[48,768]{1,0:T(8,128)(2,1)S(1)}, bf16[48,768]{1,0:T(8,128)(2,1)S(1)}, u32[]{:S(2)}, u32[]{:S(2)}) collective-permute-start(bf16[48,768]{1,0:T(8,128)(2,1)S(1)} %collective-permute-done.9), channel_id=1, source_target_pairs={{0,480},{32,0},{64,32},{96,64},{128,96},{160,128},{192,160},{224,1... | collective-permute-start | bytes 221192 | tf_op jit(solution)/shard_map/ppermute | solution.py:22
  91.4 4.1 %collective-permute-start.13 = (bf16[48,768]{1,0:T(8,128)(2,1)S(1)}, bf16[48,768]{1,0:T(8,128)(2,1)S(1)}, u32[]{:S(2)}, u32[]{:S(2)}) collective-permute-start(bf16[48,768]{1,0:T(8,128)(2,1)S(1)} %collective-permute-done.11), channel_id=1, source_target_pairs={{0,480},{32,0},{64,32},{96,64},{128,96},{160,128},{192,160},{224,1... | collective-permute-start | bytes 221192 | tf_op jit(solution)/shard_map/ppermute | solution.py:22
  96.4 4.1 %collective-permute-start.15 = (bf16[48,768]{1,0:T(8,128)(2,1)S(1)}, bf16[48,768]{1,0:T(8,128)(2,1)S(1)}, u32[]{:S(2)}, u32[]{:S(2)}) collective-permute-start(bf16[48,768]{1,0:T(8,128)(2,1)S(1)} %collective-permute-done.13), channel_id=1, source_target_pairs={{0,480},{32,0},{64,32},{96,64},{128,96},{160,128},{192,160},{224,1... | collective-permute-start | bytes 221192 | tf_op jit(solution)/shard_map/ppermute | solution.py:22
  101.4 4.8 %collective-permute-done.16 = bf16[48,768]{1,0:T(8,128)(2,1)S(1)} collective-permute-done((bf16[48,768]{1,0:T(8,128)(2,1)S(1)}, bf16[48,768]{1,0:T(8,128)(2,1)S(1)}, u32[]{:S(2)}, u32[]{:S(2)}) %collective-permute-start.16) | collective-permute-done | bytes 73760 | tf_op jit(solution)/shard_map/ppermute | solution.py:19
  112.7 2.4 fusion.82
  122.7 2.6 fusion.79
  133.0 3.0 %fusion.81 = (bf16[1,128,1,64]{3,2,1,0:T(2,128)(2,1)S(1)}, bf16[1,128,1,64]{3,2,1,0:T(2,128)(2,1)S(1)}, bf16[1,128,1,64]{3,2,1,0:T(2,128)(2,1)S(1)}, bf16[1,128,...) fusion(bf16[12,128,4,64]{3,2,1,0:T(4,128)(2,1)} %bitcast.349), kind=kLoop, calls=%fused_computation.240 | loop fusion | bytes 393216 | tf_op jit(solution)/shard_map/slice | solution.py:115
  153.7 3.3 %collective-permute-start.17 = (bf16[2,12,128,64]{2,3,1,0:T(8,128)(2,1)S(1)}, bf16[2,12,128,64]{2,3,1,0:T(8,128)(2,1)S(1)}, u32[]{:S(2)}, u32[]{:S(2)}) collective-permute-start(bf16[2,12,128,64]{2,3,1,0:T(8,128)(2,1)S(1)} %pad_maximum_fusion.2), channel_id=1, source_target_pairs={{0,1},{1,0},{2,3},{3,2},{4,5},{5,4},{6,7},{7,6},{8,9},{9,8},{10,11... | collective-permute-start | bytes 1179656 | tf_op jit(solution)/shard_map/ppermute | solution.py:53
  157.6 4.8 %collective-permute-done.17 = bf16[2,12,128,64]{2,3,1,0:T(8,128)(2,1)S(1)} collective-permute-done((bf16[2,12,128,64]{2,3,1,0:T(8,128)(2,1)S(1)}, bf16[2,12,128,64]{2,3,1,0:T(8,128)(2,1)S(1)}, u32[]{:S(2)}, u32[]{:S(2)}) %collective-permute-start.17) | collective-permute-done | bytes 393248 | tf_op jit(solution)/shard_map/ppermute | solution.py:53
  163.6 4.2 %collective-permute-start.18 = (bf16[2,12,256,64]{2,3,1,0:T(8,128)(2,1)}, bf16[2,12,256,64]{2,3,1,0:T(8,128)(2,1)}, u32[]{:S(2)}, u32[]{:S(2)}) collective-permute-start(bf16[2,12,256,64]{2,3,1,0:T(8,128)(2,1)} %maximum_select_fusion.1), channel_id=1, source_target_pairs={{0,2},{2,0},{1,3},{3,1},{4,6},{6,4},{5,7},{7,5},{8,10},{10,8},{9,1... | collective-permute-start | bytes 2359304 | tf_op jit(solution)/shard_map/ppermute | solution.py:53
  167.8 13.2 %while.10 = (s32[]{:T(128)}, f32[3,4,512]{2,1,0:T(4,128)S(1)}, f32[3,4,512]{2,1,0:T(4,128)S(1)}, f32[3,4,512,64]{2,3,1,0:T(8,128)}, pred[3,4,512]{2,1,0:T(4,128)...) while((s32[]{:T(128)}, f32[3,4,512]{2,1,0:T(4,128)S(1)}, ...), condition=%wide.region_5.6_spmd, body=%wide.region_2.5_spmd.sunk | while | flops 276965376 | bytes 14004325 | solution.py:104
  184.5 17.5 %collective-permute-done.18 = bf16[2,12,256,64]{2,3,1,0:T(8,128)(2,1)} collective-permute-done((bf16[2,12,256,64]{2,3,1,0:T(8,128)(2,1)}, bf16[2,12,256,64]{2,3,1,0:T(8,128)(2,1)}, u32[]{:S(2)}, u32[]{:S(2)}) %collective-permute-start.18) | collective-permute-done | bytes 786464 | tf_op jit(solution)/shard_map/ppermute | solution.py:53
  201.9 2.4 maximum_select_fusion
  205.6 11.3 %while.11 = (s32[]{:T(128)}, f32[3,4,128]{2,1,0:T(4,128)S(1)}, f32[3,4,128]{2,1,0:T(4,128)S(1)}, f32[3,4,128,64]{2,3,1,0:T(8,128)}, pred[3,4,512]{2,1,0:T(4,128)...) while((s32[]{:T(128)}, f32[3,4,128]{2,1,0:T(4,128)S(1)}, ...), condition=%wide.region_9.10_spmd, body=%wide.region_6.9_spmd.sunk | while | flops 68717056 | bytes 3899493 | solution.py:104
  220.0 9.4 %fusion.74 = (bf16[1,12,512,64]{3,0,1,2:T(2,128)(2,1)}, bf16[1,12,512,64]{3,0,1,2:T(2,128)(2,1)}) fusion(bf16[2,12,512,64]{3,0,1,2:T(2,128)(2,1)} %all-gather.6.cloned.1.call-done), kind=kLoop, calls=%fused_computation.233 | loop fusion | bytes 3145728 | tf_op jit(solution)/shard_map/slice | solution.py:220
  229.4 7.9 %copy.1535 = bf16[1,12,512,64]{2,3,1,0:T(8,128)(2,1)} copy(bf16[1,12,512,64]{3,0,1,2:T(2,128)(2,1)} %get-tuple-element.267) | data formatting | bytes 1572864
  237.3 7.9 %copy.1536 = bf16[1,12,512,64]{2,3,1,0:T(8,128)(2,1)} copy(bf16[1,12,512,64]{3,0,1,2:T(2,128)(2,1)} %get-tuple-element.266) | data formatting | bytes 1572864
  253.1 8.3 %fusion.52 = bf16[12,512,64]{2,1,0:T(8,128)(2,1)} fusion(f32[12,512,64]{2,1,0:T(8,128)S(1)} %bitcast.338, f32[3,4,512,64]{3,2,1,0:T(8,128)S(1)} %copy.1481, f32[12,512]{1,0:T(8,128)S(1)} %get-tuple-element.248, f32[12,16,64]{2,1,0:T(8,128)S(1)} %fusion.58, f32[12,512]{1,0:T(8,128)S(1)} %get-tuple-element.251, f32[12,512]{1,0:T(8,128)S(1)} %get-tuple-element.249, ...), kind=kLoop, calls=%fused_computation.63 | loop fusion | flops 4325376 | bytes 4116992 | tf_op jit(solution)/shard_map/convert_element_type | solution.py:237
  263.2 3.0 %fusion.57 = bf16[1,512,768]{2,1,0:T(8,128)(2,1)} fusion(bf16[512,768]{0,1:T(8,128)(2,1)S(1)} %bitcast.359, bf16[768,768]{1,0:T(8,128)(2,1)} %all-gather.8.cloned.1.call-done), kind=kOutput, calls=%fused_computation.76 | convolution fusion | flops 604372992 | bytes 2752512 | tf_op jit(solution)/shard_map/dot_general | solution.py:239
  (295 shorter events, 112.4 us)
Async XLA Ops:
  6.5 51.2 %all-gather.4.cloned.1.call-start = ((), (), s32[]{:S(2)}) async-start(), calls=%async_computation | async-start | bytes 2506752 | tf_op jit(solution)/shard_map/all_gather | solution.py:155
  7.3 212.8 %all-gather.6.cloned.1.call-start = ((), (), s32[]{:S(2)}) async-start(), calls=%async_computation.1 | async-start | bytes 3244032 | tf_op jit(solution)/shard_map/all_gather | solution.py:213
  9.3 6.2 %collective-permute-start = (bf16[6,768]{1,0:T(8,128)(2,1)S(1)}, bf16[6,768]{1,0:T(8,128)(2,1)S(1)}, u32[]{:S(2)}, u32[]{:S(2)}) collective-permute-start(bf16[6,768]{1,0:T(8,128)(2,1)S(1)} %get-tuple-element.344), channel_id=1, source_target_pairs={{0,1},{1,2},{2,3},{3,4},{4,5},{5,6},{6,7},{7,8},{8,9},{9,10},{10,1... | collective-permute-start | bytes 27656 | tf_op jit(solution)/shard_map/ppermute | solution.py:37
  14.1 5.1 %collective-permute-start.1 = (bf16[6,768]{1,0:T(8,128)(2,1)S(1)}, bf16[6,768]{1,0:T(8,128)(2,1)S(1)}, u32[]{:S(2)}, u32[]{:S(2)}) collective-permute-start(bf16[6,768]{1,0:T(8,128)(2,1)S(1)} %get-tuple-element.345), channel_id=1, source_target_pairs={{1,0},{2,1},{3,2},{4,3},{5,4},{6,5},{7,6},{8,7},{9,8},{10,9},{11,1... | collective-permute-start | bytes 27656 | tf_op jit(solution)/shard_map/ppermute | solution.py:39
  19.2 38.6 %copy-start.16 = (f32[768]{0:T(1024)S(1)}, f32[768]{0:T(1024)}, u32[]{:S(2)}) copy-start(f32[768]{0:T(1024)} %param.14) | copy-start | bytes 9220
  69.9 193.3 %all-gather.8.cloned.1.call-start = ((), (), s32[]{:S(2)}) async-start(), calls=%async_computation.2 | async-start | bytes 1253376 | tf_op jit(solution)/shard_map/all_gather | solution.py:241
  69.9 3.5 %collective-permute-start.2 = (bf16[48,768]{1,0:T(8,128)(2,1)S(1)}, bf16[48,768]{1,0:T(8,128)(2,1)S(1)}, u32[]{:S(2)}, u32[]{:S(2)}) collective-permute-start(bf16[48,768]{1,0:T(8,128)(2,1)S(1)} %copy-done.2), channel_id=1, source_target_pairs={{0,32},{32,64},{64,96},{96,128},{128,160},{160,192},{192,224},{224... | collective-permute-start | bytes 221192 | tf_op jit(solution)/shard_map/ppermute | solution.py:19
  71.1 4.1 %collective-permute-start.3 = (bf16[48,768]{1,0:T(8,128)(2,1)S(1)}, bf16[48,768]{1,0:T(8,128)(2,1)S(1)}, u32[]{:S(2)}, u32[]{:S(2)}) collective-permute-start(bf16[48,768]{1,0:T(8,128)(2,1)S(1)} %copy-done.2), channel_id=1, source_target_pairs={{0,480},{32,0},{64,32},{96,64},{128,96},{160,128},{192,160},{224,1... | collective-permute-start | bytes 221192 | tf_op jit(solution)/shard_map/ppermute | solution.py:22
  73.5 3.2 %collective-permute-start.4 = (bf16[48,768]{1,0:T(8,128)(2,1)S(1)}, bf16[48,768]{1,0:T(8,128)(2,1)S(1)}, u32[]{:S(2)}, u32[]{:S(2)}) collective-permute-start(bf16[48,768]{1,0:T(8,128)(2,1)S(1)} %collective-permute-done.2), channel_id=1, source_target_pairs={{0,32},{32,64},{64,96},{96,128},{128,160},{160,192},{192,224},{224... | collective-permute-start | bytes 221192 | tf_op jit(solution)/shard_map/ppermute | solution.py:19
  75.2 3.8 %collective-permute-start.5 = (bf16[48,768]{1,0:T(8,128)(2,1)S(1)}, bf16[48,768]{1,0:T(8,128)(2,1)S(1)}, u32[]{:S(2)}, u32[]{:S(2)}) collective-permute-start(bf16[48,768]{1,0:T(8,128)(2,1)S(1)} %collective-permute-done.3), channel_id=1, source_target_pairs={{0,480},{32,0},{64,32},{96,64},{128,96},{160,128},{192,160},{224,1... | collective-permute-start | bytes 221192 | tf_op jit(solution)/shard_map/ppermute | solution.py:22
  76.6 4.6 %collective-permute-start.6 = (bf16[48,768]{1,0:T(8,128)(2,1)S(1)}, bf16[48,768]{1,0:T(8,128)(2,1)S(1)}, u32[]{:S(2)}, u32[]{:S(2)}) collective-permute-start(bf16[48,768]{1,0:T(8,128)(2,1)S(1)} %collective-permute-done.4), channel_id=1, source_target_pairs={{0,32},{32,64},{64,96},{96,128},{128,160},{160,192},{192,224},{224... | collective-permute-start | bytes 221192 | tf_op jit(solution)/shard_map/ppermute | solution.py:19
  79.0 3.8 %collective-permute-start.7 = (bf16[48,768]{1,0:T(8,128)(2,1)S(1)}, bf16[48,768]{1,0:T(8,128)(2,1)S(1)}, u32[]{:S(2)}, u32[]{:S(2)}) collective-permute-start(bf16[48,768]{1,0:T(8,128)(2,1)S(1)} %collective-permute-done.5), channel_id=1, source_target_pairs={{0,480},{32,0},{64,32},{96,64},{128,96},{160,128},{192,160},{224,1... | collective-permute-start | bytes 221192 | tf_op jit(solution)/shard_map/ppermute | solution.py:22
  81.3 5.0 %collective-permute-start.8 = (bf16[48,768]{1,0:T(8,128)(2,1)S(1)}, bf16[48,768]{1,0:T(8,128)(2,1)S(1)}, u32[]{:S(2)}, u32[]{:S(2)}) collective-permute-start(bf16[48,768]{1,0:T(8,128)(2,1)S(1)} %collective-permute-done.6), channel_id=1, source_target_pairs={{0,32},{32,64},{64,96},{96,128},{128,160},{160,192},{192,224},{224... | collective-permute-start | bytes 221192 | tf_op jit(solution)/shard_map/ppermute | solution.py:19
  82.8 3.8 %collective-permute-start.9 = (bf16[48,768]{1,0:T(8,128)(2,1)S(1)}, bf16[48,768]{1,0:T(8,128)(2,1)S(1)}, u32[]{:S(2)}, u32[]{:S(2)}) collective-permute-start(bf16[48,768]{1,0:T(8,128)(2,1)S(1)} %collective-permute-done.7), channel_id=1, source_target_pairs={{0,480},{32,0},{64,32},{96,64},{128,96},{160,128},{192,160},{224,1... | collective-permute-start | bytes 221192 | tf_op jit(solution)/shard_map/ppermute | solution.py:22
  86.3 5.0 %collective-permute-start.10 = (bf16[48,768]{1,0:T(8,128)(2,1)S(1)}, bf16[48,768]{1,0:T(8,128)(2,1)S(1)}, u32[]{:S(2)}, u32[]{:S(2)}) collective-permute-start(bf16[48,768]{1,0:T(8,128)(2,1)S(1)} %collective-permute-done.8), channel_id=1, source_target_pairs={{0,32},{32,64},{64,96},{96,128},{128,160},{160,192},{192,224},{224... | collective-permute-start | bytes 221192 | tf_op jit(solution)/shard_map/ppermute | solution.py:19
  86.6 4.9 %collective-permute-start.11 = (bf16[48,768]{1,0:T(8,128)(2,1)S(1)}, bf16[48,768]{1,0:T(8,128)(2,1)S(1)}, u32[]{:S(2)}, u32[]{:S(2)}) collective-permute-start(bf16[48,768]{1,0:T(8,128)(2,1)S(1)} %collective-permute-done.9), channel_id=1, source_target_pairs={{0,480},{32,0},{64,32},{96,64},{128,96},{160,128},{192,160},{224,1... | collective-permute-start | bytes 221192 | tf_op jit(solution)/shard_map/ppermute | solution.py:22
  91.3 5.0 %collective-permute-start.12 = (bf16[48,768]{1,0:T(8,128)(2,1)S(1)}, bf16[48,768]{1,0:T(8,128)(2,1)S(1)}, u32[]{:S(2)}, u32[]{:S(2)}) collective-permute-start(bf16[48,768]{1,0:T(8,128)(2,1)S(1)} %collective-permute-done.10), channel_id=1, source_target_pairs={{0,32},{32,64},{64,96},{96,128},{128,160},{160,192},{192,224},{224... | collective-permute-start | bytes 221192 | tf_op jit(solution)/shard_map/ppermute | solution.py:19
  91.4 5.0 %collective-permute-start.13 = (bf16[48,768]{1,0:T(8,128)(2,1)S(1)}, bf16[48,768]{1,0:T(8,128)(2,1)S(1)}, u32[]{:S(2)}, u32[]{:S(2)}) collective-permute-start(bf16[48,768]{1,0:T(8,128)(2,1)S(1)} %collective-permute-done.11), channel_id=1, source_target_pairs={{0,480},{32,0},{64,32},{96,64},{128,96},{160,128},{192,160},{224,1... | collective-permute-start | bytes 221192 | tf_op jit(solution)/shard_map/ppermute | solution.py:22
  96.2 5.0 %collective-permute-start.14 = (bf16[48,768]{1,0:T(8,128)(2,1)S(1)}, bf16[48,768]{1,0:T(8,128)(2,1)S(1)}, u32[]{:S(2)}, u32[]{:S(2)}) collective-permute-start(bf16[48,768]{1,0:T(8,128)(2,1)S(1)} %collective-permute-done.12), channel_id=1, source_target_pairs={{0,32},{32,64},{64,96},{96,128},{128,160},{160,192},{192,224},{224... | collective-permute-start | bytes 221192 | tf_op jit(solution)/shard_map/ppermute | solution.py:19
  96.4 5.0 %collective-permute-start.15 = (bf16[48,768]{1,0:T(8,128)(2,1)S(1)}, bf16[48,768]{1,0:T(8,128)(2,1)S(1)}, u32[]{:S(2)}, u32[]{:S(2)}) collective-permute-start(bf16[48,768]{1,0:T(8,128)(2,1)S(1)} %collective-permute-done.13), channel_id=1, source_target_pairs={{0,480},{32,0},{64,32},{96,64},{128,96},{160,128},{192,160},{224,1... | collective-permute-start | bytes 221192 | tf_op jit(solution)/shard_map/ppermute | solution.py:22
  101.2 5.0 %collective-permute-start.16 = (bf16[48,768]{1,0:T(8,128)(2,1)S(1)}, bf16[48,768]{1,0:T(8,128)(2,1)S(1)}, u32[]{:S(2)}, u32[]{:S(2)}) collective-permute-start(bf16[48,768]{1,0:T(8,128)(2,1)S(1)} %collective-permute-done.14), channel_id=1, source_target_pairs={{0,32},{32,64},{64,96},{96,128},{128,160},{160,192},{192,224},{224... | collective-permute-start | bytes 221192 | tf_op jit(solution)/shard_map/ppermute | solution.py:19
  142.6 25.2 %copy-start.8 = (f32[3,4,512]{2,1,0:T(4,128)S(1)}, f32[3,4,512]{2,1,0:T(4,128)}, u32[]{:S(2)}) copy-start(f32[3,4,512]{2,1,0:T(4,128)} %custom-call.6) | copy-start | bytes 73732
  153.7 8.7 %collective-permute-start.17 = (bf16[2,12,128,64]{2,3,1,0:T(8,128)(2,1)S(1)}, bf16[2,12,128,64]{2,3,1,0:T(8,128)(2,1)S(1)}, u32[]{:S(2)}, u32[]{:S(2)}) collective-permute-start(bf16[2,12,128,64]{2,3,1,0:T(8,128)(2,1)S(1)} %pad_maximum_fusion.2), channel_id=1, source_target_pairs={{0,1},{1,0},{2,3},{3,2},{4,5},{5,4},{6,7},{7,6},{8,9},{9,8},{10,11... | collective-permute-start | bytes 1179656 | tf_op jit(solution)/shard_map/ppermute | solution.py:53
  163.6 38.3 %collective-permute-start.18 = (bf16[2,12,256,64]{2,3,1,0:T(8,128)(2,1)}, bf16[2,12,256,64]{2,3,1,0:T(8,128)(2,1)}, u32[]{:S(2)}, u32[]{:S(2)}) collective-permute-start(bf16[2,12,256,64]{2,3,1,0:T(8,128)(2,1)} %maximum_select_fusion.1), channel_id=1, source_target_pairs={{0,2},{2,0},{1,3},{3,1},{4,6},{6,4},{5,7},{7,5},{8,10},{10,8},{9,1... | collective-permute-start | bytes 2359304 | tf_op jit(solution)/shard_map/ppermute | solution.py:53
  (15 other events, 123.5 us)
Sparse Core Ops, SparseCore 0:
  9.5 48.2 all-gather.3
  70.0 80.4 all-gather.5
  152.6 41.8 all-gather.7
